TPU v7x, 32 devices: a whole 2x2x4 slice. The times are simulated.
32 devices in a mesh: groups: 2 (over y), shots: 4 (over z), dom: 2 (over x), sub: 2 (over core).
Axes of the slice: x: 2, y: 2, z: 4, core: 2. Of those that a mesh axis runs over, the one named last changes fastest.
Arguments:
- velocity: float32 [64, 16, 256], P(('groups', 'shots'), 'dom', 'sub'), parts along dimension 0, may hold values from 0.15 to 0.4
- wave_prev: bfloat16 [8, 32, 16, 256], P(('groups', 'shots'), None, 'dom', 'sub'), parts along dimension 0, may hold values from -6 to 6
- wave_now: bfloat16 [8, 32, 16, 256], P(('groups', 'shots'), None, 'dom', 'sub'), parts along dimension 0, may hold values from -6 to 6
- adj_next: bfloat16 [8, 32, 16, 256], P(('groups', 'shots'), None, 'dom', 'sub'), parts along dimension 0, may hold values from -6 to 6
- adj_now: bfloat16 [8, 32, 16, 256], P(('groups', 'shots'), None, 'dom', 'sub'), parts along dimension 0, may hold values from -6 to 6
- sponge: int32 [32, 16, 256], P(None, 'dom', 'sub'), may hold values 0 or 1
- wavelet: float32 [8, 6], P(('groups', 'shots')), parts along dimension 0, may hold values from -12 to 12
- src_pos: int32 [8], P(('groups', 'shots')), parts along dimension 0, may hold values from 0 to 4095
- rec_pos: int32 [8, 256], P(('groups', 'shots')), parts along dimension 0, may hold values from 0 to 4095
- observed: float32 [8, 4, 256], P(('groups', 'shots')), parts along dimension 0, may hold values from -6 to 6
Outputs:
- direction: float32 [64, 16, 256], P(('groups', 'shots'), 'dom', 'sub'), parts along dimension 0
- wave_out: float32 [8, 32, 16, 256], P(('groups', 'shots'), None, 'dom', 'sub'), parts along dimension 0
There are 2 independent parts, one for each index of `groups`. A program takes and returns all parts, laid end to end along the dimension named above; an argument that names none is the same for every part. Nothing has to cross between parts.
Inputs may be any that keep to these rules, and one draw needn't show every extreme that they name: `src_pos`: a horizontal position x * 256 + y on the grid. `rec_pos`: horizontal positions x * 256 + y on the grid, possibly repeated.
All inputs are finite; a program needn't handle non-finite values. Where the computation divides by a largest or mean magnitude, that divisor is 1e-20 or more. No bound on the sum of `sponge` on one device may be relied on, other than what follows from the above.
Results may differ from a plain program's by a relative error of at most 0.0003.
Values sent between devices are 32-bit elements; how exact they have to be, the bound alone decides.
A program may use at most 64 MiB of HBM per device.

v0:
```python
import jax
import jax.numpy as jnp
from jax import lax
from jax.sharding import PartitionSpec as P

NF = 4
NFIN = 2


coeffs = (-205.0 / 72.0, 8.0 / 5.0, -1.0 / 5.0, 8.0 / 315.0, -1.0 / 560.0)
damp_rate = 0.2
step_rate = 0.1
floor_share = 0.5
src_depth = 2
rec_depth = 1
reach = 4


def padded_2(cells, sides, width):
    for axis, dim in sides:
        count = lax.axis_size(axis)
        ends = count - 1
        head = lax.slice_in_dim(cells, 0, width, axis=dim)
        tail = lax.slice_in_dim(cells, cells.shape[dim] - width, cells.shape[dim], axis=dim)
        cells = jnp.concatenate(
            [
                lax.ppermute(tail, axis, [(i, (i + 1) % count) for i in range(ends)]),
                cells,
                lax.ppermute(head, axis, [((i + 1) % count, i) for i in range(ends)]),
            ],
            axis=dim,
        )
    return cells


def laplace(padded, depth, rows, cols):
    z0, x0, y0 = (reach, reach, reach)
    total = 3.0 * coeffs[0] * padded[z0 : z0 + depth, x0 : x0 + rows, y0 : y0 + cols]
    for offset in range(1, 5):
        pair = padded[z0 + offset : z0 + offset + depth, x0 : x0 + rows, y0 : y0 + cols]
        pair = pair + padded[z0 - offset : z0 - offset + depth, x0 : x0 + rows, y0 : y0 + cols]
        pair = pair + padded[z0 : z0 + depth, x0 + offset : x0 + offset + rows, y0 : y0 + cols]
        pair = pair + padded[z0 : z0 + depth, x0 - offset : x0 - offset + rows, y0 : y0 + cols]
        pair = pair + padded[z0 : z0 + depth, x0 : x0 + rows, y0 + offset : y0 + offset + cols]
        pair = pair + padded[z0 : z0 + depth, x0 : x0 + rows, y0 - offset : y0 - offset + cols]
        total = total + coeffs[offset] * pair
    return total


def advance(now, before, kappa, damp, plane, level):
    widened = padded_2(now, (("dom", 1), ("sub", 2)), 4)
    padded = jnp.pad(widened, ((reach, reach), (0, 0), (0, 0)))
    lap = laplace(padded, now.shape[0], now.shape[1], now.shape[2])
    numer = 2.0 * now - (1.0 - damp) * before + kappa * lap
    numer = numer.at[level].add(plane)
    return numer / (1.0 + damp)


def local_spots(positions, rows, cols):
    cols_all = cols * lax.axis_size("sub")
    gx = positions // cols_all
    gy = positions % cols_all
    local_x = gx - lax.axis_index("dom") * rows
    local_y = gy - lax.axis_index("sub") * cols
    inside = (local_x >= 0) & (local_x < rows) & (local_y >= 0) & (local_y < cols)
    spots = jnp.where(inside, local_x * cols + local_y, 0)
    return (spots, inside)


def place_local(spots, inside, values, rows, cols):
    kept = jnp.where(inside, values, 0.0)
    flat = jnp.zeros((rows * cols,), jnp.float32).at[spots].add(kept)
    return flat.reshape(rows, cols)


def shards(
    velocity, wave_prev, wave_now, adj_next, adj_now, sponge, wavelet, src_pos, rec_pos, observed
):
    depth, rows, cols = sponge.shape
    full_vel = lax.all_gather(velocity, "shots", axis=0, tiled=True)
    kappa = full_vel * full_vel
    damp = damp_rate * sponge.astype(jnp.float32)
    amps = wavelet[0]
    src_spot, src_inside = local_spots(src_pos, rows, cols)
    rec_spot, rec_inside = local_spots(rec_pos[0], rows, cols)
    states = [wave_prev[0].astype(jnp.float32), wave_now[0].astype(jnp.float32)]
    for step in range(NF):
        plane = place_local(src_spot, src_inside, amps[step][None], rows, cols)
        states.append(advance(states[-1], states[-2], kappa, damp, plane, src_depth))
    lam_after = adj_next[0].astype(jnp.float32)
    lam_now = adj_now[0].astype(jnp.float32)
    grad = jnp.zeros_like(kappa)
    for level in range(NF, 0, -1):
        sampled = states[level + 1][rec_depth].reshape(-1)[rec_spot]
        resid = sampled - observed[0, level - 1]
        plane = place_local(rec_spot, rec_inside, resid, rows, cols)
        lam_before = advance(lam_now, lam_after, kappa, damp, plane, rec_depth)
        lower = level - 1
        accel = states[lower + 2] - 2.0 * states[lower + 1] + states[lower]
        grad = grad + lam_before * accel
        lam_after, lam_now = (lam_now, lam_before)
    illum = jnp.zeros_like(kappa)
    for level in range(1, NF + 1):
        illum = illum + states[level + 1] * states[level + 1]
    shot_count = lax.axis_size("shots")
    grad_all, illum_all = lax.psum((grad, illum), "shots")
    precond = grad_all / (illum_all + floor_share * shot_count)
    peak = lax.pmax(jnp.max(jnp.abs(precond)), ("dom", "sub"))
    full_dir = precond / (peak + 1e-06)
    updated = full_vel * (1.0 - step_rate * full_dir)
    owned = velocity.shape[0]
    direction = lax.dynamic_slice_in_dim(full_dir, lax.axis_index("shots") * owned, owned, 0)
    kappa_new = updated * updated
    before, current = (states[-2], states[-1])
    for step in range(NFIN):
        plane = place_local(src_spot, src_inside, amps[NF + step][None], rows, cols)
        following = advance(current, before, kappa_new, damp, plane, src_depth)
        before, current = (current, following)
    return (direction, current[None])


def solution(mesh):
    return jax.shard_map(
        shards,
        mesh=mesh,
        in_specs=(
            P(("groups", "shots"), "dom", "sub"),
            P(("groups", "shots"), None, "dom", "sub"),
            P(("groups", "shots"), None, "dom", "sub"),
            P(("groups", "shots"), None, "dom", "sub"),
            P(("groups", "shots"), None, "dom", "sub"),
            P(None, "dom", "sub"),
            P(("groups", "shots"), None),
            P(("groups", "shots")),
            P(("groups", "shots"), None),
            P(("groups", "shots"), None, None),
        ),
        out_specs=(
            P(("groups", "shots"), "dom", "sub"),
            P(("groups", "shots"), None, "dom", "sub"),
        ),
        check_vma=False,
    )
```

profile of v0, /device:TPU:1, one launch (start us, length us, event | category | flops | bytes accessed | tf_op | source)
XLA Modules:
  0.0 231.4 jit_solution(6835556315163786703)
XLA Ops:
  8.1 3.9 %collective-permute-start.4 = (f32[32,4,128]{2,1,0:T(4,128)S(1)}, f32[32,4,128]{2,1,0:T(4,128)S(1)}, u32[]{:S(2)}, u32[]{:S(2)}) collective-permute-start(f32[32,4,128]{2,1,0:T(4,128)S(1)} %get-tuple-element.261), channel_id=1, source_target_pairs={{0,2},{1,3},{4,6},{5,7},{8,10},{9,11},{12,14},{13,15},{16,18},{17,... | collective-permute-start | bytes 196616 | tf_op jit(solution)/shard_map/ppermute | solution.py:27
  12.1 1.3 collective-permute-start.5
  13.4 4.0 %collective-permute-start = (f32[32,4,128]{2,1,0:T(4,128)S(1)}, f32[32,4,128]{2,1,0:T(4,128)S(1)}, u32[]{:S(2)}, u32[]{:S(2)}) collective-permute-start(f32[32,4,128]{2,1,0:T(4,128)S(1)} %get-tuple-element.251), channel_id=1, source_target_pairs={{0,2},{1,3},{4,6},{5,7},{8,10},{9,11},{12,14},{13,15},{16,18},{17,... | collective-permute-start | bytes 196616 | tf_op jit(solution)/shard_map/ppermute | solution.py:27
  17.4 1.3 collective-permute-start.1
  21.9 1.2 compare_and_fusion.1
  25.5 2.6 %fusion.344 = f32[1024]{0:T(1024)S(1)} fusion(f32[1024]{0:T(1024)S(1)} %broadcast.395.clone, s32[]{:T(128)} %bitcast.12, pred[1]{0:T(512)(128)(4,1)} %get-tuple-element.275, f32[1,1]{1,0:T(1,128)} %get-tuple-element.270, s32[1]{0:T(128)} %compare_select_fusion.1), kind=kLoop, calls=%fused_computation.685 | loop fusion | flops 5 | bytes 525 | tf_op jit(solution)/shard_map/scatter-add | solution.py:72
  28.1 2.6 %fusion.342 = f32[1024]{0:T(1024)S(1)} fusion(f32[1024]{0:T(1024)S(1)} %broadcast.395.clone.1, s32[]{:T(128)} %bitcast.12, pred[1]{0:T(512)(128)(4,1)} %get-tuple-element.275, f32[1,1]{1,0:T(1,128)} %get-tuple-element.269, s32[1]{0:T(128)} %compare_select_fusion.1), kind=kLoop, calls=%fused_computation.682 | loop fusion | flops 5 | bytes 525 | tf_op jit(solution)/shard_map/scatter-add | solution.py:72
  30.8 2.6 %fusion.340 = f32[1024]{0:T(1024)S(1)} fusion(f32[1024]{0:T(1024)S(1)} %broadcast.395.clone.2, s32[]{:T(128)} %bitcast.12, pred[1]{0:T(512)(128)(4,1)} %get-tuple-element.275, f32[1,1]{1,0:T(1,128)} %get-tuple-element.268, s32[1]{0:T(128)} %compare_select_fusion.1), kind=kLoop, calls=%fused_computation.679 | loop fusion | flops 5 | bytes 525 | tf_op jit(solution)/shard_map/scatter-add | solution.py:72
  33.4 2.6 %fusion.338 = f32[1024]{0:T(1024)S(1)} fusion(f32[1024]{0:T(1024)S(1)} %broadcast.395.clone.3, s32[]{:T(128)} %bitcast.12, pred[1]{0:T(512)(128)(4,1)} %get-tuple-element.275, f32[1,1]{1,0:T(1,128)} %get-tuple-element.267, s32[1]{0:T(128)} %compare_select_fusion.1), kind=kLoop, calls=%fused_computation.676 | loop fusion | flops 5 | bytes 525 | tf_op jit(solution)/shard_map/scatter-add | solution.py:72
  36.0 10.7 %all_gather.3 = f32[32,8,128]{2,1,0:T(8,128)S(1)} all-gather(f32[8,8,128]{2,1,0:T(8,128)S(1)} %copy-done.7), channel_id=1, replica_groups=mesh['groups'=2,'shots'=4,'dom'=2,'sub'=2] {'shots'}, dimensions={0}, use_global_device_ids=true | all-gather | bytes 163840 | tf_op jit(solution)/shard_map/all_gather | solution.py:80
  46.9 1.3 collective-permute-start.6
  48.2 6.3 %collective-permute-start.7 = (f32[32,16,4]{2,1,0:T(8,128)S(1)}, f32[32,16,4]{2,1,0:T(8,128)S(1)}, u32[]{:S(2)}, u32[]{:S(2)}) collective-permute-start(f32[32,16,4]{2,1,0:T(8,128)S(1)} %get-tuple-element.240), channel_id=1, source_target_pairs={{1,0},{3,2},{5,4},{7,6},{9,8},{11,10},{13,12},{15,14},{17,16},{19,... | collective-permute-start | bytes 24584 | tf_op jit(solution)/shard_map/ppermute | solution.py:29
  54.8 1.3 collective-permute-start.2
  56.1 3.1 %collective-permute-start.3 = (f32[32,16,4]{2,1,0:T(8,128)S(1)}, f32[32,16,4]{2,1,0:T(8,128)S(1)}, u32[]{:S(2)}, u32[]{:S(2)}) collective-permute-start(f32[32,16,4]{2,1,0:T(8,128)S(1)} %get-tuple-element.220), channel_id=1, source_target_pairs={{1,0},{3,2},{5,4},{7,6},{9,8},{11,10},{13,12},{15,14},{17,16},{19,... | collective-permute-start | bytes 24584 | tf_op jit(solution)/shard_map/ppermute | solution.py:29
  61.1 4.3 %collective-permute-start.8 = (f32[32,4,128]{2,1,0:T(4,128)S(1)}, f32[32,4,128]{2,1,0:T(4,128)S(1)}, u32[]{:S(2)}, u32[]{:S(2)}) collective-permute-start(f32[32,4,128]{2,1,0:T(4,128)S(1)} %get-tuple-element.259), channel_id=1, source_target_pairs={{0,2},{1,3},{4,6},{5,7},{8,10},{9,11},{12,14},{13,15},{16,18},{17,... | collective-permute-start | bytes 196616 | tf_op jit(solution)/shard_map/ppermute | solution.py:27
  65.4 1.3 collective-permute-start.9
  67.5 3.8 %collective-permute-done.9 = f32[32,4,128]{2,1,0:T(4,128)S(1)} collective-permute-done((f32[32,4,128]{2,1,0:T(4,128)S(1)}, f32[32,4,128]{2,1,0:T(4,128)S(1)}, u32[]{:S(2)}, u32[]{:S(2)}) %collective-permute-start.9) | collective-permute-done | bytes 65568 | tf_op jit(solution)/shard_map/ppermute | solution.py:29
  71.5 1.3 collective-permute-start.10
  72.8 3.1 %collective-permute-start.11 = (f32[32,16,4]{2,1,0:T(8,128)S(1)}, f32[32,16,4]{2,1,0:T(8,128)S(1)}, u32[]{:S(2)}, u32[]{:S(2)}) collective-permute-start(f32[32,16,4]{2,1,0:T(8,128)S(1)} %get-tuple-element.236), channel_id=1, source_target_pairs={{1,0},{3,2},{5,4},{7,6},{9,8},{11,10},{13,12},{15,14},{17,16},{19,... | collective-permute-start | bytes 24584 | tf_op jit(solution)/shard_map/ppermute | solution.py:29
  78.5 1.3 collective-permute-start.12
  79.8 1.3 collective-permute-start.13
  81.1 1.4 gather_fusion.3
  82.5 2.3 %collective-permute-done.13 = f32[32,4,128]{2,1,0:T(4,128)S(1)} collective-permute-done((f32[32,4,128]{2,1,0:T(4,128)S(1)}, f32[32,4,128]{2,1,0:T(4,128)S(1)}, u32[]{:S(2)}, u32[]{:S(2)}) %collective-permute-start.13) | collective-permute-done | bytes 65568 | tf_op jit(solution)/shard_map/ppermute | solution.py:29
  85.0 1.3 collective-permute-start.14
  86.3 3.6 %collective-permute-start.15 = (f32[32,16,4]{2,1,0:T(8,128)S(1)}, f32[32,16,4]{2,1,0:T(8,128)S(1)}, u32[]{:S(2)}, u32[]{:S(2)}) collective-permute-start(f32[32,16,4]{2,1,0:T(8,128)S(1)} %get-tuple-element.232), channel_id=1, source_target_pairs={{1,0},{3,2},{5,4},{7,6},{9,8},{11,10},{13,12},{15,14},{17,16},{19,... | collective-permute-start | bytes 24584 | tf_op jit(solution)/shard_map/ppermute | solution.py:29
  92.5 1.3 collective-permute-start.16
  93.8 1.3 collective-permute-start.17
  95.1 1.4 gather_fusion.2
  96.5 2.3 %collective-permute-done.17 = f32[32,4,128]{2,1,0:T(4,128)S(1)} collective-permute-done((f32[32,4,128]{2,1,0:T(4,128)S(1)}, f32[32,4,128]{2,1,0:T(4,128)S(1)}, u32[]{:S(2)}, u32[]{:S(2)}) %collective-permute-start.17) | collective-permute-done | bytes 65568 | tf_op jit(solution)/shard_map/ppermute | solution.py:29
  99.0 1.3 collective-permute-start.18
  100.3 3.9 %collective-permute-start.19 = (f32[32,16,4]{2,1,0:T(8,128)S(1)}, f32[32,16,4]{2,1,0:T(8,128)S(1)}, u32[]{:S(2)}, u32[]{:S(2)}) collective-permute-start(f32[32,16,4]{2,1,0:T(8,128)S(1)} %get-tuple-element.228), channel_id=1, source_target_pairs={{1,0},{3,2},{5,4},{7,6},{9,8},{11,10},{13,12},{15,14},{17,16},{19,... | collective-permute-start | bytes 24584 | tf_op jit(solution)/shard_map/ppermute | solution.py:29
  104.2 1.4 gather_fusion.1
  107.7 1.4 gather_fusion
  109.1 2.3 %scatter_custom_fusion = f32[1024]{0:T(1024)S(1)} fusion(s32[256]{0:T(256)S(1)} %bitcast.109, f32[256]{0:T(256)S(1)} %get-tuple-element.274, f32[]{:T(128)} %constant.405.clone.1), kind=kCustom, calls=%fused_computation.646 | custom fusion | flops 256 | bytes 4100 | tf_op jit(solution)/shard_map/scatter-add | solution.py:72
  111.5 1.3 collective-permute-start.20
  112.8 1.3 collective-permute-start.21
  114.3 3.8 %collective-permute-done.21 = f32[32,4,128]{2,1,0:T(4,128)S(1)} collective-permute-done((f32[32,4,128]{2,1,0:T(4,128)S(1)}, f32[32,4,128]{2,1,0:T(4,128)S(1)}, u32[]{:S(2)}, u32[]{:S(2)}) %collective-permute-start.21) | collective-permute-done | bytes 65568 | tf_op jit(solution)/shard_map/ppermute | solution.py:29
  118.4 1.3 collective-permute-start.22
  119.7 3.1 %collective-permute-start.23 = (f32[32,16,4]{2,1,0:T(8,128)S(1)}, f32[32,16,4]{2,1,0:T(8,128)S(1)}, u32[]{:S(2)}, u32[]{:S(2)}) collective-permute-start(f32[32,16,4]{2,1,0:T(8,128)S(1)} %get-tuple-element.216), channel_id=1, source_target_pairs={{1,0},{3,2},{5,4},{7,6},{9,8},{11,10},{13,12},{15,14},{17,16},{19,... | collective-permute-start | bytes 24584 | tf_op jit(solution)/shard_map/ppermute | solution.py:29
  122.7 2.3 %scatter_custom_fusion.1 = f32[1024]{0:T(1024)S(1)} fusion(s32[256]{0:T(256)S(1)} %bitcast.110, f32[256]{0:T(256)S(1)} %get-tuple-element.273, f32[]{:T(128)} %constant.405.clone.1), kind=kCustom, calls=%fused_computation.644 | custom fusion | flops 256 | bytes 4100 | tf_op jit(solution)/shard_map/scatter-add | solution.py:72
  126.5 1.3 collective-permute-start.24
  127.8 1.3 collective-permute-start.25
  129.5 4.3 %collective-permute-done.25 = f32[32,4,128]{2,1,0:T(4,128)S(1)} collective-permute-done((f32[32,4,128]{2,1,0:T(4,128)S(1)}, f32[32,4,128]{2,1,0:T(4,128)S(1)}, u32[]{:S(2)}, u32[]{:S(2)}) %collective-permute-start.25) | collective-permute-done | bytes 65568 | tf_op jit(solution)/shard_map/ppermute | solution.py:29
  134.0 1.3 collective-permute-start.26
  135.3 3.1 %collective-permute-start.27 = (f32[32,16,4]{2,1,0:T(8,128)S(1)}, f32[32,16,4]{2,1,0:T(8,128)S(1)}, u32[]{:S(2)}, u32[]{:S(2)}) collective-permute-start(f32[32,16,4]{2,1,0:T(8,128)S(1)} %get-tuple-element.212), channel_id=1, source_target_pairs={{1,0},{3,2},{5,4},{7,6},{9,8},{11,10},{13,12},{15,14},{17,16},{19,... | collective-permute-start | bytes 24584 | tf_op jit(solution)/shard_map/ppermute | solution.py:29
  138.3 2.3 %scatter_custom_fusion.3 = f32[1024]{0:T(1024)S(1)} fusion(s32[256]{0:T(256)S(1)} %bitcast.111, f32[256]{0:T(256)S(1)} %get-tuple-element.200, f32[]{:T(128)} %constant.405.clone.1), kind=kCustom, calls=%fused_computation.640 | custom fusion | flops 256 | bytes 4100 | tf_op jit(solution)/shard_map/scatter-add | solution.py:72
  140.6 2.3 %scatter_custom_fusion.2 = f32[1024]{0:T(1024)S(1)} fusion(s32[256]{0:T(256)S(1)} %bitcast.112, f32[256]{0:T(256)S(1)} %get-tuple-element.272, f32[]{:T(128)} %constant.405.clone.1), kind=kCustom, calls=%fused_computation.642 | custom fusion | flops 256 | bytes 4100 | tf_op jit(solution)/shard_map/scatter-add | solution.py:72
  144.5 1.3 collective-permute-start.28
  145.8 1.3 collective-permute-start.29
  147.1 4.0 %collective-permute-start.32 = (f32[32,4,128]{2,1,0:T(4,128)S(1)}, f32[32,4,128]{2,1,0:T(4,128)S(1)}, u32[]{:S(2)}, u32[]{:S(2)}) collective-permute-start(f32[32,4,128]{2,1,0:T(4,128)S(1)} %get-tuple-element.253), channel_id=1, source_target_pairs={{0,2},{1,3},{4,6},{5,7},{8,10},{9,11},{12,14},{13,15},{16,18},{17,... | collective-permute-start | bytes 196616 | tf_op jit(solution)/shard_map/ppermute | solution.py:27
  151.1 1.3 collective-permute-start.33
  152.6 1.3 collective-permute-start.30
  153.9 3.3 %collective-permute-start.31 = (f32[32,16,4]{2,1,0:T(8,128)S(1)}, f32[32,16,4]{2,1,0:T(8,128)S(1)}, u32[]{:S(2)}, u32[]{:S(2)}) collective-permute-start(f32[32,16,4]{2,1,0:T(8,128)S(1)} %get-tuple-element.208), channel_id=1, source_target_pairs={{1,0},{3,2},{5,4},{7,6},{9,8},{11,10},{13,12},{15,14},{17,16},{19,... | collective-permute-start | bytes 24584 | tf_op jit(solution)/shard_map/ppermute | solution.py:29
  160.5 1.3 collective-permute-start.34
  161.8 3.1 %collective-permute-start.35 = (f32[32,16,4]{2,1,0:T(8,128)S(1)}, f32[32,16,4]{2,1,0:T(8,128)S(1)}, u32[]{:S(2)}, u32[]{:S(2)}) collective-permute-start(f32[32,16,4]{2,1,0:T(8,128)S(1)} %get-tuple-element.224), channel_id=1, source_target_pairs={{1,0},{3,2},{5,4},{7,6},{9,8},{11,10},{13,12},{15,14},{17,16},{19,... | collective-permute-start | bytes 24584 | tf_op jit(solution)/shard_map/ppermute | solution.py:29
  164.8 2.6 %fusion.336 = f32[1024]{0:T(1024)S(1)} fusion(f32[1024]{0:T(1024)S(1)} %broadcast.395.clone.4, s32[]{:T(128)} %bitcast.12, pred[1]{0:T(512)(128)(4,1)} %get-tuple-element.275, f32[1,1]{1,0:T(1,128)} %get-tuple-element.271, s32[1]{0:T(128)} %compare_select_fusion.1), kind=kLoop, calls=%fused_computation.673 | loop fusion | flops 5 | bytes 525 | tf_op jit(solution)/shard_map/scatter-add | solution.py:72
  167.8 27.8 %all-reduce.13.cloned.1.call-done = (f32[32,8,128]{2,1,0:T(8,128)}, f32[32,8,128]{2,1,0:T(8,128)}) async-done(((f32[32,8,128]{2,1,0:T(8,128)}, f32[32,8,128]{2,1,0:T(8,128)}), (f32[32,8,128]{2,1,0:T(8,128)}, f32[32,8,128]{2,1,0:T(8,128)})) %all-reduce.13.cloned.1.call-update) | async-done | bytes 262160 | tf_op jit(solution)/shard_map/psum | solution.py:106
  195.5 1.6 abs_reduce_fusion
  197.6 8.5 %pmax.7 = f32[]{:T(128)} all-reduce(f32[]{:T(128)} %abs_reduce_fusion), channel_id=1, replica_groups=mesh['groups'=2,'shots'=4,'dom'=2,'sub'=2] {'dom','sub'}, use_global_device_ids=true, to_apply=%region_7.8 | all-reduce | flops 1 | bytes 8 | tf_op jit(solution)/shard_map/pmax | solution.py:108
  207.5 3.1 %collective-permute-start.36 = (f32[32,4,128]{2,1,0:T(4,128)S(1)}, f32[32,4,128]{2,1,0:T(4,128)S(1)}, u32[]{:S(2)}, u32[]{:S(2)}) collective-permute-start(f32[32,4,128]{2,1,0:T(4,128)S(1)} %get-tuple-element.243), channel_id=1, source_target_pairs={{0,2},{1,3},{4,6},{5,7},{8,10},{9,11},{12,14},{13,15},{16,18},{17,... | collective-permute-start | bytes 196616 | tf_op jit(solution)/shard_map/ppermute | solution.py:27
  210.6 1.3 collective-permute-start.37
  211.9 2.6 %fusion.334 = f32[1024]{0:T(1024)S(1)} fusion(f32[1024]{0:T(1024)S(1)} %broadcast.395.clone.5, s32[]{:T(128)} %bitcast.12, pred[1]{0:T(512)(128)(4,1)} %get-tuple-element.275, f32[1,1]{1,0:T(1,128)} %get-tuple-element.266, s32[1]{0:T(128)} %compare_select_fusion.1), kind=kLoop, calls=%fused_computation.670 | loop fusion | flops 5 | bytes 525 | tf_op jit(solution)/shard_map/scatter-add | solution.py:72
  215.8 1.3 collective-permute-start.38
  217.1 4.3 %collective-permute-start.39 = (f32[32,16,4]{2,1,0:T(8,128)S(1)}, f32[32,16,4]{2,1,0:T(8,128)S(1)}, u32[]{:S(2)}, u32[]{:S(2)}) collective-permute-start(f32[32,16,4]{2,1,0:T(8,128)S(1)} %get-tuple-element.204), channel_id=1, source_target_pairs={{1,0},{3,2},{5,4},{7,6},{9,8},{11,10},{13,12},{15,14},{17,16},{19,... | collective-permute-start | bytes 24584 | tf_op jit(solution)/shard_map/ppermute | solution.py:29
  (158 shorter events, 26.9 us)
Async XLA Ops:
  7.2 188.4 %all-reduce.13.cloned.1.call-start = ((), (), s32[]{:S(2)}) async-start(), calls=%async_computation | async-start | bytes 524288 | tf_op jit(solution)/shard_map/psum | solution.py:106
  8.1 5.3 %copy-start.4 = (bf16[1,32,8,128]{3,2,1,0:T(8,128)(2,1)S(1)}, bf16[1,32,8,128]{3,2,1,0:T(8,128)(2,1)}, u32[]{:S(2)}) copy-start(bf16[1,32,8,128]{3,2,1,0:T(8,128)(2,1)} %param.46) | copy-start | bytes 196612
  8.1 38.6 %collective-permute-start.4 = (f32[32,4,128]{2,1,0:T(4,128)S(1)}, f32[32,4,128]{2,1,0:T(4,128)S(1)}, u32[]{:S(2)}, u32[]{:S(2)}) collective-permute-start(f32[32,4,128]{2,1,0:T(4,128)S(1)} %get-tuple-element.261), channel_id=1, source_target_pairs={{0,2},{1,3},{4,6},{5,7},{8,10},{9,11},{12,14},{13,15},{16,18},{17,... | collective-permute-start | bytes 196616 | tf_op jit(solution)/shard_map/ppermute | solution.py:27
  12.1 34.7 %collective-permute-start.5 = (f32[32,4,128]{2,1,0:T(4,128)S(1)}, f32[32,4,128]{2,1,0:T(4,128)S(1)}, u32[]{:S(2)}, u32[]{:S(2)}) collective-permute-start(f32[32,4,128]{2,1,0:T(4,128)S(1)} %get-tuple-element.260), channel_id=1, source_target_pairs={{2,0},{3,1},{6,4},{7,5},{10,8},{11,9},{14,12},{15,13},{18,16},{19,... | collective-permute-start | bytes 196616 | tf_op jit(solution)/shard_map/ppermute | solution.py:29
  13.4 41.1 %collective-permute-start = (f32[32,4,128]{2,1,0:T(4,128)S(1)}, f32[32,4,128]{2,1,0:T(4,128)S(1)}, u32[]{:S(2)}, u32[]{:S(2)}) collective-permute-start(f32[32,4,128]{2,1,0:T(4,128)S(1)} %get-tuple-element.251), channel_id=1, source_target_pairs={{0,2},{1,3},{4,6},{5,7},{8,10},{9,11},{12,14},{13,15},{16,18},{17,... | collective-permute-start | bytes 196616 | tf_op jit(solution)/shard_map/ppermute | solution.py:27
  17.4 37.1 %collective-permute-start.1 = (f32[32,4,128]{2,1,0:T(4,128)S(1)}, f32[32,4,128]{2,1,0:T(4,128)S(1)}, u32[]{:S(2)}, u32[]{:S(2)}) collective-permute-start(f32[32,4,128]{2,1,0:T(4,128)S(1)} %get-tuple-element.250), channel_id=1, source_target_pairs={{2,0},{3,1},{6,4},{7,5},{10,8},{11,9},{14,12},{15,13},{18,16},{19,... | collective-permute-start | bytes 196616 | tf_op jit(solution)/shard_map/ppermute | solution.py:29
  18.7 0.7 copy-start.8
  18.7 1.3 copy-start.9
  20.0 0.7 copy-start.10
  20.7 15.3 %copy-start.7 = (f32[8,8,128]{2,1,0:T(8,128)S(1)}, f32[8,8,128]{2,1,0:T(8,128)}, u32[]{:S(2)}) copy-start(f32[8,8,128]{2,1,0:T(8,128)} %param.42) | copy-start | bytes 98308
  46.9 12.2 %collective-permute-start.6 = (f32[32,16,4]{2,1,0:T(8,128)S(1)}, f32[32,16,4]{2,1,0:T(8,128)S(1)}, u32[]{:S(2)}, u32[]{:S(2)}) collective-permute-start(f32[32,16,4]{2,1,0:T(8,128)S(1)} %get-tuple-element.241), channel_id=1, source_target_pairs={{0,1},{2,3},{4,5},{6,7},{8,9},{10,11},{12,13},{14,15},{16,17},{18,... | collective-permute-start | bytes 24584 | tf_op jit(solution)/shard_map/ppermute | solution.py:27
  48.2 10.9 %collective-permute-start.7 = (f32[32,16,4]{2,1,0:T(8,128)S(1)}, f32[32,16,4]{2,1,0:T(8,128)S(1)}, u32[]{:S(2)}, u32[]{:S(2)}) collective-permute-start(f32[32,16,4]{2,1,0:T(8,128)S(1)} %get-tuple-element.240), channel_id=1, source_target_pairs={{1,0},{3,2},{5,4},{7,6},{9,8},{11,10},{13,12},{15,14},{17,16},{19,... | collective-permute-start | bytes 24584 | tf_op jit(solution)/shard_map/ppermute | solution.py:29
  54.8 12.0 %collective-permute-start.2 = (f32[32,16,4]{2,1,0:T(8,128)S(1)}, f32[32,16,4]{2,1,0:T(8,128)S(1)}, u32[]{:S(2)}, u32[]{:S(2)}) collective-permute-start(f32[32,16,4]{2,1,0:T(8,128)S(1)} %get-tuple-element.221), channel_id=1, source_target_pairs={{0,1},{2,3},{4,5},{6,7},{8,9},{10,11},{12,13},{14,15},{16,17},{18,... | collective-permute-start | bytes 24584 | tf_op jit(solution)/shard_map/ppermute | solution.py:27
  56.1 10.7 %collective-permute-start.3 = (f32[32,16,4]{2,1,0:T(8,128)S(1)}, f32[32,16,4]{2,1,0:T(8,128)S(1)}, u32[]{:S(2)}, u32[]{:S(2)}) collective-permute-start(f32[32,16,4]{2,1,0:T(8,128)S(1)} %get-tuple-element.220), channel_id=1, source_target_pairs={{1,0},{3,2},{5,4},{7,6},{9,8},{11,10},{13,12},{15,14},{17,16},{19,... | collective-permute-start | bytes 24584 | tf_op jit(solution)/shard_map/ppermute | solution.py:29
  59.5 0.9 copy-start
  59.5 0.9 copy-start.1
  59.5 0.9 copy-start.5
  61.1 6.4 %collective-permute-start.8 = (f32[32,4,128]{2,1,0:T(4,128)S(1)}, f32[32,4,128]{2,1,0:T(4,128)S(1)}, u32[]{:S(2)}, u32[]{:S(2)}) collective-permute-start(f32[32,4,128]{2,1,0:T(4,128)S(1)} %get-tuple-element.259), channel_id=1, source_target_pairs={{0,2},{1,3},{4,6},{5,7},{8,10},{9,11},{12,14},{13,15},{16,18},{17,... | collective-permute-start | bytes 196616 | tf_op jit(solution)/shard_map/ppermute | solution.py:27
  65.4 5.9 %collective-permute-start.9 = (f32[32,4,128]{2,1,0:T(4,128)S(1)}, f32[32,4,128]{2,1,0:T(4,128)S(1)}, u32[]{:S(2)}, u32[]{:S(2)}) collective-permute-start(f32[32,4,128]{2,1,0:T(4,128)S(1)} %get-tuple-element.258), channel_id=1, source_target_pairs={{2,0},{3,1},{6,4},{7,5},{10,8},{11,9},{14,12},{15,13},{18,16},{19,... | collective-permute-start | bytes 196616 | tf_op jit(solution)/shard_map/ppermute | solution.py:29
  71.3 4.5 %copy-start.6 = (bf16[1,32,8,128]{3,2,1,0:T(8,128)(2,1)S(1)}, bf16[1,32,8,128]{3,2,1,0:T(8,128)(2,1)}, u32[]{:S(2)}) copy-start(bf16[1,32,8,128]{3,2,1,0:T(8,128)(2,1)} %param.45) | copy-start | bytes 196612
  71.5 5.0 %collective-permute-start.10 = (f32[32,16,4]{2,1,0:T(8,128)S(1)}, f32[32,16,4]{2,1,0:T(8,128)S(1)}, u32[]{:S(2)}, u32[]{:S(2)}) collective-permute-start(f32[32,16,4]{2,1,0:T(8,128)S(1)} %get-tuple-element.237), channel_id=1, source_target_pairs={{0,1},{2,3},{4,5},{6,7},{8,9},{10,11},{12,13},{14,15},{16,17},{18,... | collective-permute-start | bytes 24584 | tf_op jit(solution)/shard_map/ppermute | solution.py:27
  72.8 4.2 %collective-permute-start.11 = (f32[32,16,4]{2,1,0:T(8,128)S(1)}, f32[32,16,4]{2,1,0:T(8,128)S(1)}, u32[]{:S(2)}, u32[]{:S(2)}) collective-permute-start(f32[32,16,4]{2,1,0:T(8,128)S(1)} %get-tuple-element.236), channel_id=1, source_target_pairs={{1,0},{3,2},{5,4},{7,6},{9,8},{11,10},{13,12},{15,14},{17,16},{19,... | collective-permute-start | bytes 24584 | tf_op jit(solution)/shard_map/ppermute | solution.py:29
  78.5 4.0 %collective-permute-start.12 = (f32[32,4,128]{2,1,0:T(4,128)S(1)}, f32[32,4,128]{2,1,0:T(4,128)S(1)}, u32[]{:S(2)}, u32[]{:S(2)}) collective-permute-start(f32[32,4,128]{2,1,0:T(4,128)S(1)} %get-tuple-element.257), channel_id=1, source_target_pairs={{0,2},{1,3},{4,6},{5,7},{8,10},{9,11},{12,14},{13,15},{16,18},{17,... | collective-permute-start | bytes 196616 | tf_op jit(solution)/shard_map/ppermute | solution.py:27
  79.8 5.0 %collective-permute-start.13 = (f32[32,4,128]{2,1,0:T(4,128)S(1)}, f32[32,4,128]{2,1,0:T(4,128)S(1)}, u32[]{:S(2)}, u32[]{:S(2)}) collective-permute-start(f32[32,4,128]{2,1,0:T(4,128)S(1)} %get-tuple-element.256), channel_id=1, source_target_pairs={{2,0},{3,1},{6,4},{7,5},{10,8},{11,9},{14,12},{15,13},{18,16},{19,... | collective-permute-start | bytes 196616 | tf_op jit(solution)/shard_map/ppermute | solution.py:29
  85.0 4.9 %collective-permute-start.14 = (f32[32,16,4]{2,1,0:T(8,128)S(1)}, f32[32,16,4]{2,1,0:T(8,128)S(1)}, u32[]{:S(2)}, u32[]{:S(2)}) collective-permute-start(f32[32,16,4]{2,1,0:T(8,128)S(1)} %get-tuple-element.233), channel_id=1, source_target_pairs={{0,1},{2,3},{4,5},{6,7},{8,9},{10,11},{12,13},{14,15},{16,17},{18,... | collective-permute-start | bytes 24584 | tf_op jit(solution)/shard_map/ppermute | solution.py:27
  86.3 4.8 %collective-permute-start.15 = (f32[32,16,4]{2,1,0:T(8,128)S(1)}, f32[32,16,4]{2,1,0:T(8,128)S(1)}, u32[]{:S(2)}, u32[]{:S(2)}) collective-permute-start(f32[32,16,4]{2,1,0:T(8,128)S(1)} %get-tuple-element.232), channel_id=1, source_target_pairs={{1,0},{3,2},{5,4},{7,6},{9,8},{11,10},{13,12},{15,14},{17,16},{19,... | collective-permute-start | bytes 24584 | tf_op jit(solution)/shard_map/ppermute | solution.py:29
  92.5 4.0 %collective-permute-start.16 = (f32[32,4,128]{2,1,0:T(4,128)S(1)}, f32[32,4,128]{2,1,0:T(4,128)S(1)}, u32[]{:S(2)}, u32[]{:S(2)}) collective-permute-start(f32[32,4,128]{2,1,0:T(4,128)S(1)} %get-tuple-element.255), channel_id=1, source_target_pairs={{0,2},{1,3},{4,6},{5,7},{8,10},{9,11},{12,14},{13,15},{16,18},{17,... | collective-permute-start | bytes 196616 | tf_op jit(solution)/shard_map/ppermute | solution.py:27
  93.8 5.0 %collective-permute-start.17 = (f32[32,4,128]{2,1,0:T(4,128)S(1)}, f32[32,4,128]{2,1,0:T(4,128)S(1)}, u32[]{:S(2)}, u32[]{:S(2)}) collective-permute-start(f32[32,4,128]{2,1,0:T(4,128)S(1)} %get-tuple-element.254), channel_id=1, source_target_pairs={{2,0},{3,1},{6,4},{7,5},{10,8},{11,9},{14,12},{15,13},{18,16},{19,... | collective-permute-start | bytes 196616 | tf_op jit(solution)/shard_map/ppermute | solution.py:29
  99.0 6.6 %collective-permute-start.18 = (f32[32,16,4]{2,1,0:T(8,128)S(1)}, f32[32,16,4]{2,1,0:T(8,128)S(1)}, u32[]{:S(2)}, u32[]{:S(2)}) collective-permute-start(f32[32,16,4]{2,1,0:T(8,128)S(1)} %get-tuple-element.229), channel_id=1, source_target_pairs={{0,1},{2,3},{4,5},{6,7},{8,9},{10,11},{12,13},{14,15},{16,17},{18,... | collective-permute-start | bytes 24584 | tf_op jit(solution)/shard_map/ppermute | solution.py:27
  100.3 5.3 %collective-permute-start.19 = (f32[32,16,4]{2,1,0:T(8,128)S(1)}, f32[32,16,4]{2,1,0:T(8,128)S(1)}, u32[]{:S(2)}, u32[]{:S(2)}) collective-permute-start(f32[32,16,4]{2,1,0:T(8,128)S(1)} %get-tuple-element.228), channel_id=1, source_target_pairs={{1,0},{3,2},{5,4},{7,6},{9,8},{11,10},{13,12},{15,14},{17,16},{19,... | collective-permute-start | bytes 24584 | tf_op jit(solution)/shard_map/ppermute | solution.py:29
  111.5 2.8 %collective-permute-start.20 = (f32[32,4,128]{2,1,0:T(4,128)S(1)}, f32[32,4,128]{2,1,0:T(4,128)S(1)}, u32[]{:S(2)}, u32[]{:S(2)}) collective-permute-start(f32[32,4,128]{2,1,0:T(4,128)S(1)} %get-tuple-element.249), channel_id=1, source_target_pairs={{0,2},{1,3},{4,6},{5,7},{8,10},{9,11},{12,14},{13,15},{16,18},{17,... | collective-permute-start | bytes 196616 | tf_op jit(solution)/shard_map/ppermute | solution.py:27
  112.8 5.3 %collective-permute-start.21 = (f32[32,4,128]{2,1,0:T(4,128)S(1)}, f32[32,4,128]{2,1,0:T(4,128)S(1)}, u32[]{:S(2)}, u32[]{:S(2)}) collective-permute-start(f32[32,4,128]{2,1,0:T(4,128)S(1)} %get-tuple-element.248), channel_id=1, source_target_pairs={{2,0},{3,1},{6,4},{7,5},{10,8},{11,9},{14,12},{15,13},{18,16},{19,... | collective-permute-start | bytes 196616 | tf_op jit(solution)/shard_map/ppermute | solution.py:29
  118.4 6.7 %collective-permute-start.22 = (f32[32,16,4]{2,1,0:T(8,128)S(1)}, f32[32,16,4]{2,1,0:T(8,128)S(1)}, u32[]{:S(2)}, u32[]{:S(2)}) collective-permute-start(f32[32,16,4]{2,1,0:T(8,128)S(1)} %get-tuple-element.217), channel_id=1, source_target_pairs={{0,1},{2,3},{4,5},{6,7},{8,9},{10,11},{12,13},{14,15},{16,17},{18,... | collective-permute-start | bytes 24584 | tf_op jit(solution)/shard_map/ppermute | solution.py:27
  119.7 5.4 %collective-permute-start.23 = (f32[32,16,4]{2,1,0:T(8,128)S(1)}, f32[32,16,4]{2,1,0:T(8,128)S(1)}, u32[]{:S(2)}, u32[]{:S(2)}) collective-permute-start(f32[32,16,4]{2,1,0:T(8,128)S(1)} %get-tuple-element.216), channel_id=1, source_target_pairs={{1,0},{3,2},{5,4},{7,6},{9,8},{11,10},{13,12},{15,14},{17,16},{19,... | collective-permute-start | bytes 24584 | tf_op jit(solution)/shard_map/ppermute | solution.py:29
  126.5 3.0 %collective-permute-start.24 = (f32[32,4,128]{2,1,0:T(4,128)S(1)}, f32[32,4,128]{2,1,0:T(4,128)S(1)}, u32[]{:S(2)}, u32[]{:S(2)}) collective-permute-start(f32[32,4,128]{2,1,0:T(4,128)S(1)} %get-tuple-element.247), channel_id=1, source_target_pairs={{0,2},{1,3},{4,6},{5,7},{8,10},{9,11},{12,14},{13,15},{16,18},{17,... | collective-permute-start | bytes 196616 | tf_op jit(solution)/shard_map/ppermute | solution.py:27
  127.8 5.9 %collective-permute-start.25 = (f32[32,4,128]{2,1,0:T(4,128)S(1)}, f32[32,4,128]{2,1,0:T(4,128)S(1)}, u32[]{:S(2)}, u32[]{:S(2)}) collective-permute-start(f32[32,4,128]{2,1,0:T(4,128)S(1)} %get-tuple-element.246), channel_id=1, source_target_pairs={{2,0},{3,1},{6,4},{7,5},{10,8},{11,9},{14,12},{15,13},{18,16},{19,... | collective-permute-start | bytes 196616 | tf_op jit(solution)/shard_map/ppermute | solution.py:29
  134.0 9.0 %collective-permute-start.26 = (f32[32,16,4]{2,1,0:T(8,128)S(1)}, f32[32,16,4]{2,1,0:T(8,128)S(1)}, u32[]{:S(2)}, u32[]{:S(2)}) collective-permute-start(f32[32,16,4]{2,1,0:T(8,128)S(1)} %get-tuple-element.213), channel_id=1, source_target_pairs={{0,1},{2,3},{4,5},{6,7},{8,9},{10,11},{12,13},{14,15},{16,17},{18,... | collective-permute-start | bytes 24584 | tf_op jit(solution)/shard_map/ppermute | solution.py:27
  135.3 7.7 %collective-permute-start.27 = (f32[32,16,4]{2,1,0:T(8,128)S(1)}, f32[32,16,4]{2,1,0:T(8,128)S(1)}, u32[]{:S(2)}, u32[]{:S(2)}) collective-permute-start(f32[32,16,4]{2,1,0:T(8,128)S(1)} %get-tuple-element.212), channel_id=1, source_target_pairs={{1,0},{3,2},{5,4},{7,6},{9,8},{11,10},{13,12},{15,14},{17,16},{19,... | collective-permute-start | bytes 24584 | tf_op jit(solution)/shard_map/ppermute | solution.py:29
  144.5 7.9 %collective-permute-start.28 = (f32[32,4,128]{2,1,0:T(4,128)S(1)}, f32[32,4,128]{2,1,0:T(4,128)S(1)}, u32[]{:S(2)}, u32[]{:S(2)}) collective-permute-start(f32[32,4,128]{2,1,0:T(4,128)S(1)} %get-tuple-element.245), channel_id=1, source_target_pairs={{0,2},{1,3},{4,6},{5,7},{8,10},{9,11},{12,14},{13,15},{16,18},{17,... | collective-permute-start | bytes 196616 | tf_op jit(solution)/shard_map/ppermute | solution.py:27
  145.8 6.6 %collective-permute-start.29 = (f32[32,4,128]{2,1,0:T(4,128)S(1)}, f32[32,4,128]{2,1,0:T(4,128)S(1)}, u32[]{:S(2)}, u32[]{:S(2)}) collective-permute-start(f32[32,4,128]{2,1,0:T(4,128)S(1)} %get-tuple-element.244), channel_id=1, source_target_pairs={{2,0},{3,1},{6,4},{7,5},{10,8},{11,9},{14,12},{15,13},{18,16},{19,... | collective-permute-start | bytes 196616 | tf_op jit(solution)/shard_map/ppermute | solution.py:29
  147.1 10.1 %collective-permute-start.32 = (f32[32,4,128]{2,1,0:T(4,128)S(1)}, f32[32,4,128]{2,1,0:T(4,128)S(1)}, u32[]{:S(2)}, u32[]{:S(2)}) collective-permute-start(f32[32,4,128]{2,1,0:T(4,128)S(1)} %get-tuple-element.253), channel_id=1, source_target_pairs={{0,2},{1,3},{4,6},{5,7},{8,10},{9,11},{12,14},{13,15},{16,18},{17,... | collective-permute-start | bytes 196616 | tf_op jit(solution)/shard_map/ppermute | solution.py:27
  151.1 6.1 %collective-permute-start.33 = (f32[32,4,128]{2,1,0:T(4,128)S(1)}, f32[32,4,128]{2,1,0:T(4,128)S(1)}, u32[]{:S(2)}, u32[]{:S(2)}) collective-permute-start(f32[32,4,128]{2,1,0:T(4,128)S(1)} %get-tuple-element.252), channel_id=1, source_target_pairs={{2,0},{3,1},{6,4},{7,5},{10,8},{11,9},{14,12},{15,13},{18,16},{19,... | collective-permute-start | bytes 196616 | tf_op jit(solution)/shard_map/ppermute | solution.py:29
  152.6 4.7 %collective-permute-start.30 = (f32[32,16,4]{2,1,0:T(8,128)S(1)}, f32[32,16,4]{2,1,0:T(8,128)S(1)}, u32[]{:S(2)}, u32[]{:S(2)}) collective-permute-start(f32[32,16,4]{2,1,0:T(8,128)S(1)} %get-tuple-element.209), channel_id=1, source_target_pairs={{0,1},{2,3},{4,5},{6,7},{8,9},{10,11},{12,13},{14,15},{16,17},{18,... | collective-permute-start | bytes 24584 | tf_op jit(solution)/shard_map/ppermute | solution.py:27
  153.9 4.2 %collective-permute-start.31 = (f32[32,16,4]{2,1,0:T(8,128)S(1)}, f32[32,16,4]{2,1,0:T(8,128)S(1)}, u32[]{:S(2)}, u32[]{:S(2)}) collective-permute-start(f32[32,16,4]{2,1,0:T(8,128)S(1)} %get-tuple-element.208), channel_id=1, source_target_pairs={{1,0},{3,2},{5,4},{7,6},{9,8},{11,10},{13,12},{15,14},{17,16},{19,... | collective-permute-start | bytes 24584 | tf_op jit(solution)/shard_map/ppermute | solution.py:29
  160.5 6.9 %collective-permute-start.34 = (f32[32,16,4]{2,1,0:T(8,128)S(1)}, f32[32,16,4]{2,1,0:T(8,128)S(1)}, u32[]{:S(2)}, u32[]{:S(2)}) collective-permute-start(f32[32,16,4]{2,1,0:T(8,128)S(1)} %get-tuple-element.225), channel_id=1, source_target_pairs={{0,1},{2,3},{4,5},{6,7},{8,9},{10,11},{12,13},{14,15},{16,17},{18,... | collective-permute-start | bytes 24584 | tf_op jit(solution)/shard_map/ppermute | solution.py:27
  161.8 5.6 %collective-permute-start.35 = (f32[32,16,4]{2,1,0:T(8,128)S(1)}, f32[32,16,4]{2,1,0:T(8,128)S(1)}, u32[]{:S(2)}, u32[]{:S(2)}) collective-permute-start(f32[32,16,4]{2,1,0:T(8,128)S(1)} %get-tuple-element.224), channel_id=1, source_target_pairs={{1,0},{3,2},{5,4},{7,6},{9,8},{11,10},{13,12},{15,14},{17,16},{19,... | collective-permute-start | bytes 24584 | tf_op jit(solution)/shard_map/ppermute | solution.py:29
  197.1 9.6 %copy-start.2 = (f32[32,8,128]{2,1,0:T(8,128)S(1)}, f32[32,8,128]{2,1,0:T(8,128)}, u32[]{:S(2)}) copy-start(f32[32,8,128]{2,1,0:T(8,128)} %get-tuple-element.194) | copy-start | bytes 393220
  197.1 9.6 %copy-start.3 = (f32[32,8,128]{2,1,0:T(8,128)S(1)}, f32[32,8,128]{2,1,0:T(8,128)}, u32[]{:S(2)}) copy-start(f32[32,8,128]{2,1,0:T(8,128)} %get-tuple-element.195) | copy-start | bytes 393220
  207.5 7.1 %collective-permute-start.36 = (f32[32,4,128]{2,1,0:T(4,128)S(1)}, f32[32,4,128]{2,1,0:T(4,128)S(1)}, u32[]{:S(2)}, u32[]{:S(2)}) collective-permute-start(f32[32,4,128]{2,1,0:T(4,128)S(1)} %get-tuple-element.243), channel_id=1, source_target_pairs={{0,2},{1,3},{4,6},{5,7},{8,10},{9,11},{12,14},{13,15},{16,18},{17,... | collective-permute-start | bytes 196616 | tf_op jit(solution)/shard_map/ppermute | solution.py:27
  210.6 5.0 %collective-permute-start.37 = (f32[32,4,128]{2,1,0:T(4,128)S(1)}, f32[32,4,128]{2,1,0:T(4,128)S(1)}, u32[]{:S(2)}, u32[]{:S(2)}) collective-permute-start(f32[32,4,128]{2,1,0:T(4,128)S(1)} %get-tuple-element.242), channel_id=1, source_target_pairs={{2,0},{3,1},{6,4},{7,5},{10,8},{11,9},{14,12},{15,13},{18,16},{19,... | collective-permute-start | bytes 196616 | tf_op jit(solution)/shard_map/ppermute | solution.py:29
  215.8 6.2 %collective-permute-start.38 = (f32[32,16,4]{2,1,0:T(8,128)S(1)}, f32[32,16,4]{2,1,0:T(8,128)S(1)}, u32[]{:S(2)}, u32[]{:S(2)}) collective-permute-start(f32[32,16,4]{2,1,0:T(8,128)S(1)} %get-tuple-element.205), channel_id=1, source_target_pairs={{0,1},{2,3},{4,5},{6,7},{8,9},{10,11},{12,13},{14,15},{16,17},{18,... | collective-permute-start | bytes 24584 | tf_op jit(solution)/shard_map/ppermute | solution.py:27
  217.1 5.4 %collective-permute-start.39 = (f32[32,16,4]{2,1,0:T(8,128)S(1)}, f32[32,16,4]{2,1,0:T(8,128)S(1)}, u32[]{:S(2)}, u32[]{:S(2)}) collective-permute-start(f32[32,16,4]{2,1,0:T(8,128)S(1)} %get-tuple-element.204), channel_id=1, source_target_pairs={{1,0},{3,2},{5,4},{7,6},{9,8},{11,10},{13,12},{15,14},{17,16},{19,... | collective-permute-start | bytes 24584 | tf_op jit(solution)/shard_map/ppermute | solution.py:29
Sparse Core Ops, SparseCore 0:
  160.5 35.0 all-reduce.12
where the time goes:
time: 233 us; the launch traced here: 231 us
  starting transfers between devices  88.3 us (38%)
  waiting for transfers between devices  48.9 us (21%)
  other arithmetic  45.3 us (19%)
  between operations  19.5 us (8%)
  blocking collectives  19.2 us (8%)
  local copies, waits for them, and re-layouts  10.1 us (4%)
    ppermute x20, starting transfers between devices, padded_2(): lax.ppermute(head, axis, [((i + 1) % count, i) for i in range(ends)])  49.6 us
    ppermute x20, starting transfers between devices, padded_2(): lax.ppermute(tail, axis, [(i, (i + 1) % count) for i in range(ends)])  38.7 us
    psum x1, waiting for transfers between devices, shards(): grad_all, illum_all = lax.psum((grad, illum), 'shots')  27.8 us
    scatter-add x10, other arithmetic, place_local(): flat = jnp.zeros((rows * cols,), jnp.float32).at[spots].add(kept)  24.9 us
    ppermute x20, waiting for transfers between devices, padded_2(): lax.ppermute(head, axis, [((i + 1) % count, i) for i in range(ends)])  20.5 us
    all_gather x1, blocking collectives, shards(): full_vel = lax.all_gather(velocity, 'shots', axis=0, tiled=True)  10.7 us
    pmax x1, blocking collectives, shards(): peak = lax.pmax(jnp.max(jnp.abs(precond)), ('dom', 'sub'))  8.54 us
    concatenate x30, other arithmetic, padded_2(): jnp.concatenate([lax.ppermute(tail, axis, [(i, (i + 1) % count) for i in...  8.09 us
  transfers between devices with their start and end apart: 41, of which 13 were waited for; matrix products, arithmetic and copies ran while one was open for 14% of the time, Pallas kernels for 0%

commit v1 on v0

v1 whole, which is shorter than its diff:
```python
import functools

import jax
import jax.numpy as jnp
import numpy as np
from jax import lax
from jax.experimental import pallas as pl
from jax.experimental.pallas import tpu as pltpu
from jax.sharding import PartitionSpec as P

NF = 4
NFIN = 2

coeffs = (-205.0 / 72.0, 8.0 / 5.0, -1.0 / 5.0, 8.0 / 315.0, -1.0 / 560.0)
damp_rate = 0.2
step_rate = 0.1
floor_share = 0.5
src_depth = 2
rec_depth = 1
reach = 4

MESH = pl.DeviceIdType.MESH
F32 = jnp.float32
BF16 = jnp.bfloat16


def band(size, period):
    full = np.zeros((size, size), np.float64)
    for row in range(size):
        for k in range(1, reach + 1):
            for col in (row - k, row + k):
                if 0 <= col < size and col // period == row // period:
                    full[row, col] = coeffs[k]
    high = full.astype(np.float32).astype(BF16)
    low = (full - high.astype(np.float64)).astype(np.float32).astype(BF16)
    return high, low


def split(value):
    high = value.astype(BF16)
    low = (value - high.astype(F32)).astype(BF16)
    return high, low


def copies_needed(shots, dom, sub):
    fields = 5 * ((dom - 1) + dom * (sub - 1))
    slabs = 2 * (shots * dom * sub)
    return fields + slabs + shots


def kernel(
    sizes,
    vel_ref, prev_ref, now_ref, adjn_ref, adj_ref, sponge_ref, amp_ref, src_ref, rec_ref, obs_ref,
    bh_ref, bl_ref, kh_ref, kl_ref,
    dir_ref, out_ref,
    U, L, V, SP, IV, QV, KP, ACC, PC, OB, CNT, GI, GR, ss, rs,
):
    shots, dom, sub, depth, rows, cols, owned, zb = sizes
    X, Y = dom * rows, sub * cols
    s = lax.axis_index("shots")
    d = lax.axis_index("dom")
    c = lax.axis_index("sub")
    counts = {"shots": shots, "dom": dom, "sub": sub}
    me = {"shots": s, "dom": d, "sub": c}
    tickets = [0]
    sent = []

    def peer(axis, j):
        return lax.rem(me[axis] + j, counts[axis])

    def source(axis, j):
        return lax.rem(me[axis] + (counts[axis] - j), counts[axis])

    def xs(i):
        return pl.ds(pl.multiple_of(i * rows, rows), rows)

    def ys(i):
        return pl.ds(pl.multiple_of(i * cols, cols), cols)

    def send(src, dst, axis, j):
        idx = tickets[0]
        tickets[0] += 1
        copy = pltpu.make_async_remote_copy(
            src_ref=src, dst_ref=dst, send_sem=ss.at[idx], recv_sem=rs.at[idx],
            device_id={axis: peer(axis, j)}, device_id_type=MESH,
        )
        copy.start()
        sent.append(copy)
        return idx

    def arrived(idx, dst, axis):
        pltpu.make_async_remote_copy(
            src_ref=dst, dst_ref=dst, send_sem=ss.at[idx], recv_sem=rs.at[idx],
            device_id={axis: peer(axis, 1)}, device_id_type=MESH,
        ).wait_recv()

    def field_send(place):
        hops = [(i, send(place(d, c), place(d, c), "dom", i)) for i in range(1, dom)]
        cross = [(0, k, send(place(d, c), place(d, c), "sub", k)) for k in range(1, sub)]
        return hops, cross

    def field_relay(place, state):
        hops, cross = state
        for i, idx in hops:
            here = place(source("dom", i), c)
            arrived(idx, here, "dom")
            cross += [(i, k, send(here, here, "sub", k)) for k in range(1, sub)]

    def field_done(place, state):
        for i, k, idx in state[1]:
            arrived(idx, place(source("dom", i), source("sub", k)), "sub")

    def slab_send(place, first, second):
        own = place({"shots": s, "dom": d}, c)
        state = {
            "one": [(i, send(own, own, first, i)) for i in range(1, counts[first])],
            "two": [(0, j, send(own, own, second, j)) for j in range(1, counts[second])],
            "cross": [(0, 0, k, send(own, own, "sub", k)) for k in range(1, sub)],
        }
        return state

    def slab_relay(place, state, first, second):
        for i, idx in state["one"]:
            here = place({first: source(first, i), second: me[second]}, c)
            arrived(idx, here, first)
            state["two"] += [(i, j, send(here, here, second, j)) for j in range(1, counts[second])]
            state["cross"] += [(i, 0, k, send(here, here, "sub", k)) for k in range(1, sub)]
        for i, j, idx in state["two"]:
            here = place({first: source(first, i), second: source(second, j)}, c)
            arrived(idx, here, second)
            state["cross"] += [(i, j, k, send(here, here, "sub", k)) for k in range(1, sub)]

    def slab_done(place, state, first, second):
        for i, j, k, idx in state["cross"]:
            arrived(idx, place({first: source(first, i), second: source(second, j)}, source("sub", k)), "sub")

    def in_field(ref, n):
        return lambda i, k: ref.at[n, pl.ds(reach, depth), xs(i), ys(k)]

    def in_whole(ref):
        return lambda i, k: ref.at[:, xs(i), ys(k)]

    def in_slab(ref):
        return lambda at, k: ref.at[pl.ds(at["shots"] * owned, owned), xs(at["dom"]), ys(k)]

    barrier = pltpu.get_barrier_semaphore()
    for axis, count in counts.items():
        for j in range(1, count):
            pl.semaphore_signal(barrier, inc=1, device_id={axis: peer(axis, j)}, device_id_type=MESH)

    own_x, own_y = xs(d), ys(c)
    V[pl.ds(s * owned, owned), own_x, own_y] = vel_ref[...]
    U[1, pl.ds(reach, depth), own_x, own_y] = now_ref[0].astype(F32)
    U[0, pl.ds(reach, depth), own_x, own_y] = prev_ref[0].astype(F32)
    SP[:, own_x, own_y] = sponge_ref[...].astype(F32)
    L[1, pl.ds(reach, depth), own_x, own_y] = adj_ref[0].astype(F32)
    L[0, pl.ds(reach, depth), own_x, own_y] = adjn_ref[0].astype(F32)

    pl.semaphore_wait(barrier, sum(counts.values()) - 3)

    vel_state = slab_send(in_slab(V), "dom", "shots")
    now_state = field_send(in_field(U, 1))
    sp_state = field_send(in_whole(SP))
    prev_state = field_send(in_field(U, 0))
    adj_state = field_send(in_field(L, 1))
    adjn_state = field_send(in_field(L, 0))

    edge = jnp.zeros((reach, X, Y), F32)
    for ref in (U, L):
        for n in range(ref.shape[0]):
            ref[n, 0:reach] = edge
            ref[n, reach + depth : 2 * reach + depth] = edge
    pos = rec_ref[...]
    row_of = jnp.zeros_like(pos)
    for x in range(1, X):
        row_of = row_of + (pos >= x * Y).astype(jnp.int32)
    col_of = pos - row_of * Y
    nrec = pos.shape[1]
    x_hot = (lax.broadcasted_iota(jnp.int32, (X, nrec), 0) == row_of).astype(F32)
    y_hot = (lax.broadcasted_iota(jnp.int32, (Y, nrec), 0) == col_of).astype(F32).astype(BF16)

    def spread(lhs):
        return lax.dot_general(lhs, y_hot, (((1,), (1,)), ((), ())), preferred_element_type=F32)

    CNT[...] = spread(x_hot.astype(BF16))
    for n in range(NF):
        vals = x_hot * obs_ref[0, n : n + 1, :]
        a, rest = split(vals)
        b, rest2 = split(vals - a.astype(F32))
        del rest
        OB[n] = spread(a) + spread(b) + spread(rest2)
    flat = lax.broadcasted_iota(jnp.int32, (X, Y), 0) * Y + lax.broadcasted_iota(jnp.int32, (X, Y), 1)
    src_hot = (flat == src_ref[0]).astype(F32)

    slab_relay(in_slab(V), vel_state, "dom", "shots")
    field_relay(in_field(U, 1), now_state)
    field_relay(in_whole(SP), sp_state)
    field_relay(in_field(U, 0), prev_state)
    slab_done(in_slab(V), vel_state, "dom", "shots")
    field_done(in_whole(SP), sp_state)
    for z in range(depth):
        damp = damp_rate * SP[z]
        inv = 1.0 / (1.0 + damp)
        IV[z] = inv
        QV[z] = (1.0 - damp) * inv
        vel = V[z]
        KP[z] = vel * vel * inv
    field_done(in_field(U, 1), now_state)
    field_done(in_field(U, 0), prev_state)

    def lateral(ref, n):
        for b in range(depth // zb):
            lo = reach + b * zb
            u = ref[n, lo : lo + zb].reshape(zb * X, Y)
            uh, ul = split(u)
            acc = jnp.dot(uh, bh_ref[...], preferred_element_type=F32)
            acc = acc + jnp.dot(kh_ref[...], uh, preferred_element_type=F32)
            acc = acc + jnp.dot(uh, bl_ref[...], preferred_element_type=F32)
            acc = acc + jnp.dot(ul, bh_ref[...], preferred_element_type=F32)
            acc = acc + jnp.dot(kl_ref[...], uh, preferred_element_type=F32)
            acc = acc + jnp.dot(kh_ref[...], ul, preferred_element_type=F32)
            ACC[b * zb : (b + 1) * zb] = acc.reshape(zb, X, Y)

    def level(ref, n, z, xr, yr, plane):
        mid = ref[n, reach + z, xr, yr]
        lap = ACC[z, xr, yr] + (3.0 * coeffs[0]) * mid
        for k in range(1, reach + 1):
            lap = lap + coeffs[k] * (ref[n, reach + z + k, xr, yr] + ref[n, reach + z - k, xr, yr])
        inv = IV[z, xr, yr]
        drive = 2.0 * mid if plane is None else 2.0 * mid + plane
        return inv * drive - QV[z, xr, yr] * ref[n - 1, reach + z, xr, yr] + KP[z, xr, yr] * lap

    whole_x, whole_y = slice(None), slice(None)

    def advance(ref, n, plane, at):
        lateral(ref, n)
        for z in range(depth):
            ref[n + 1, reach + z] = level(ref, n, z, whole_x, whole_y, plane if z == at else None)

    for n in range(NF):
        advance(U, n + 1, src_hot * amp_ref[0, n], src_depth)
        if n == 0:
            field_relay(in_field(L, 1), adj_state)
        if n == 1:
            field_relay(in_field(L, 0), adjn_state)
    field_done(in_field(L, 1), adj_state)
    field_done(in_field(L, 0), adjn_state)

    for n in range(NF, 0, -1):
        plane = CNT[...] * U[n + 1, reach + rec_depth] - OB[n - 1]
        advance(L, NF + 1 - n, plane, rec_depth)

    for z in range(depth):
        at = (reach + z, own_x, own_y)
        u = [U[(n,) + at] for n in range(NF + 2)]
        grad = None
        illum = None
        for n in range(NF):
            term = L[(NF + 1 - n,) + at] * (u[n + 2] - 2.0 * u[n + 1] + u[n])
            grad = term if grad is None else grad + term
            square = u[n + 2] * u[n + 2]
            illum = square if illum is None else illum + square
        GI[0, z] = grad
        GI[1, z] = illum

    parts = []
    for j in range(1, shots):
        to = peer("shots", j)
        parts.append(send(GI.at[:, pl.ds(to * owned, owned)], GR.at[j - 1], "shots", j))
    lateral(U, NF + 1)
    total = GI[:, pl.ds(s * owned, owned)]
    for j in range(1, shots):
        arrived(parts[j - 1], GR.at[j - 1], "shots")
        total = total + GR[j - 1]
    mine = total[0] / (total[1] + floor_share * shots)
    PC[pl.ds(s * owned, owned), own_x, own_y] = mine
    pc_state = slab_send(in_slab(PC), "shots", "dom")
    slab_relay(in_slab(PC), pc_state, "shots", "dom")
    slab_done(in_slab(PC), pc_state, "shots", "dom")
    top = jnp.abs(PC[0])
    for z in range(1, depth):
        top = jnp.maximum(top, jnp.abs(PC[z]))
    peak = jnp.max(jnp.max(top, axis=0, keepdims=True), axis=1, keepdims=True)
    scale = 1.0 / (peak + 1e-06)
    dir_ref[...] = mine * scale
    for z in range(depth):
        updated = V[z] * (1.0 - step_rate * (PC[z] * scale))
        KP[z] = updated * updated * IV[z]
    for n in range(NFIN):
        plane = src_hot * amp_ref[0, NF + n]
        if n > 0:
            lateral(U, NF + 1 + n)
        if n < NFIN - 1:
            for z in range(depth):
                U[NF + 2 + n, reach + z] = level(
                    U, NF + 1 + n, z, whole_x, whole_y, plane if z == src_depth else None
                )
        else:
            for z in range(depth):
                out_ref[0, z] = level(U, NF + 1 + n, z, own_x, own_y, None)
            ACC[0] = plane * IV[src_depth]
            out_ref[0, src_depth] += ACC[0, own_x, own_y]
    for copy in sent:
        copy.wait_send()


def solution(mesh):
    shots, dom, sub = mesh.shape["shots"], mesh.shape["dom"], mesh.shape["sub"]

    def shards(velocity, wave_prev, wave_now, adj_next, adj_now, sponge, wavelet, src_pos, rec_pos, observed):
        depth, rows, cols = sponge.shape
        owned = velocity.shape[0]
        X, Y = dom * rows, sub * cols
        zb = min(depth, max(1, 256 // X))
        bh, bl = band(Y, Y)
        kh, kl = band(zb * X, X)
        vm = pl.BlockSpec(memory_space=pltpu.VMEM)
        sm = pl.BlockSpec(memory_space=pltpu.SMEM)
        whole = pltpu.VMEM((depth, X, Y), F32)
        n_sems = copies_needed(shots, dom, sub)
        return tuple(pl.pallas_call(
            functools.partial(kernel, (shots, dom, sub, depth, rows, cols, owned, zb)),
            out_shape=(
                jax.ShapeDtypeStruct((owned, rows, cols), F32),
                jax.ShapeDtypeStruct((1, depth, rows, cols), F32),
            ),
            in_specs=[vm] * 6 + [sm, sm] + [vm] * 6,
            out_specs=(vm, vm),
            scratch_shapes=[
                pltpu.VMEM((NF + NFIN + 1, depth + 2 * reach, X, Y), F32),
                pltpu.VMEM((NF + 2, depth + 2 * reach, X, Y), F32),
                whole, whole, whole, whole, whole, whole, whole,
                pltpu.VMEM((NF, X, Y), F32),
                pltpu.VMEM((X, Y), F32),
                pltpu.VMEM((2, depth, rows, cols), F32),
                pltpu.VMEM((max(1, shots - 1), 2, owned, rows, cols), F32),
                pltpu.SemaphoreType.DMA((n_sems,)),
                pltpu.SemaphoreType.DMA((n_sems,)),
            ],
            compiler_params=pltpu.CompilerParams(
                collective_id=0, has_side_effects=True, vmem_limit_bytes=56 * 1024 * 1024
            ),
        )(velocity, wave_prev, wave_now, adj_next, adj_now, sponge, wavelet, src_pos, rec_pos, observed,
          jnp.asarray(bh), jnp.asarray(bl), jnp.asarray(kh), jnp.asarray(kl)))

    return jax.shard_map(
        shards,
        mesh=mesh,
        in_specs=(
            P(("groups", "shots"), "dom", "sub"),
            P(("groups", "shots"), None, "dom", "sub"),
            P(("groups", "shots"), None, "dom", "sub"),
            P(("groups", "shots"), None, "dom", "sub"),
            P(("groups", "shots"), None, "dom", "sub"),
            P(None, "dom", "sub"),
            P(("groups", "shots"), None),
            P(("groups", "shots")),
            P(("groups", "shots"), None),
            P(("groups", "shots"), None, None),
        ),
        out_specs=(
            P(("groups", "shots"), "dom", "sub"),
            P(("groups", "shots"), None, "dom", "sub"),
        ),
        check_vma=False,
    )
```

time: 233 us -> 51.6 us (0.22)
  starting transfers between devices: 88.3 us -> 0 us
  waiting for transfers between devices: 48.9 us -> 0 us
  Pallas kernels: 0 us -> 47.2 us
  other arithmetic: 45.3 us -> 0 us
  blocking collectives: 19.2 us -> 0 us
  between operations: 19.5 us -> 1.29 us
  local copies, waits for them, and re-layouts: 10.1 us -> 2.94 us
    ppermute x40 -> x0, starting transfers between devices: 88.3 us -> none  [the longest x20 49.6 us: padded_2(): lax.ppermute(head, axis, [((i + 1) % count, i) for i in range(ends)])]
    pallas_call x0 -> x1, Pallas kernels: none -> 47.2 us  [shards(): pl.pallas_call(functools.partial(kernel, (shots, dom, sub, depth, rows, c...]
    psum x1 -> x0, waiting for transfers between devices: 27.8 us -> none  [shards(): grad_all, illum_all = lax.psum((grad, illum), 'shots')]
    scatter-add x20 -> x0, other arithmetic: 25 us -> none  [the longest x10 24.9 us: place_local(): flat = jnp.zeros((rows * cols,), jnp.float32).at[spots].add(kept)]
    ppermute x40 -> x0, waiting for transfers between devices: 21.1 us -> none  [the longest x20 20.5 us: padded_2(): lax.ppermute(head, axis, [((i + 1) % count, i) for i in range(ends)])]
    all_gather x1 -> x0, blocking collectives: 10.7 us -> none  [shards(): full_vel = lax.all_gather(velocity, 'shots', axis=0, tiled=True)]
    pmax x1 -> x0, blocking collectives: 8.54 us -> none  [shards(): peak = lax.pmax(jnp.max(jnp.abs(precond)), ('dom', 'sub'))]
    concatenate x30 -> x0, other arithmetic: 8.09 us -> none  [padded_2(): jnp.concatenate([lax.ppermute(tail, axis, [(i, (i + 1) % count) for i in...]
  transfers between devices with their start and end apart: 41 -> 0, of which waited for: 13 -> 0; matrix products, arithmetic and copies ran while one was open for 14% -> 0% of each run, Pallas kernels for 0% -> 0%
where the time goes in v1:
time: 51.6 us; the launch traced here: 51.4 us
  Pallas kernels  47.2 us (91%)
  local copies, waits for them, and re-layouts  2.94 us (6%)
  between operations  1.29 us (2%)
    pallas_call x1, Pallas kernels, shards(): pl.pallas_call(functools.partial(kernel, (shots, dom, sub, depth, rows, c...  47.2 us
    unnamed x2, local copies, waits for them, and re-layouts  2.94 us

profile of v1, /device:TPU:1, one launch (start us, length us, event | category | flops | bytes accessed | tf_op | source)
XLA Modules:
  0.0 51.4 jit_solution(9995163956427446163)
XLA Ops:
  1.3 47.2 %shard_map.149 = (f32[8,8,128]{2,1,0:T(8,128)}, f32[1,32,8,128]{3,2,1,0:T(8,128)}) custom-call(f32[8,8,128]{2,1,0:T(8,128)} %vel_ref.1, bf16[1,32,8,128]{3,2,1,0:T(8,128)(2,1)} %prev_ref.1, bf16[1,32,8,128]{3,2,1,0:T(8,128)(2,1)} %now_ref.1, bf16[1,32,8,128]{3,2,1,0:T(8,128)(2,1)} %adjn_ref.1, bf16[1,32,8,128]{3,2,1,0:T(8,128)(2,1)} %adj_ref.1, ...), custom_call_target="tpu_custom_call" | custom-call | tf_op jit(solution)/shard_map/pallas_call | solution.py:321
  48.5 1.4 %copy.19 = f32[8,8,128]{2,1,0:T(8,128)} copy(f32[8,8,128]{2,1,0:T(8,128)} %get-tuple-element.4) | data formatting | bytes 65536
  49.8 1.6 %copy.20 = f32[1,32,8,128]{3,2,1,0:T(8,128)} copy(f32[1,32,8,128]{3,2,1,0:T(8,128)} %get-tuple-element.5) | data formatting | bytes 262144

commit v2 on v1

--- a/solution.py
+++ b/solution.py
@@ -45,14 +45,14 @@
 def copies_needed(shots, dom, sub):
     fields = 5 * ((dom - 1) + dom * (sub - 1))
     slabs = 2 * (shots * dom * sub)
-    return fields + slabs + shots
+    return fields + slabs + 2 * shots
 
 
 def kernel(
     sizes,
     vel_ref, prev_ref, now_ref, adjn_ref, adj_ref, sponge_ref, amp_ref, src_ref, rec_ref, obs_ref,
     bh_ref, bl_ref, kh_ref, kl_ref,
-    dir_ref, out_ref,
+    both_ref,
     U, L, V, SP, IV, QV, KP, ACC, PC, OB, CNT, GI, GR, ss, rs,
 ):
     shots, dom, sub, depth, rows, cols, owned, zb = sizes
@@ -125,6 +125,8 @@
             arrived(idx, here, first)
             state["two"] += [(i, j, send(here, here, second, j)) for j in range(1, counts[second])]
             state["cross"] += [(i, 0, k, send(here, here, "sub", k)) for k in range(1, sub)]
+
+    def slab_relay_two(place, state, first, second):
         for i, j, idx in state["two"]:
             here = place({first: source(first, i), second: source(second, j)}, c)
             arrived(idx, here, second)
@@ -142,6 +144,19 @@
 
     def in_slab(ref):
         return lambda at, k: ref.at[pl.ds(at["shots"] * owned, owned), xs(at["dom"]), ys(k)]
+
+    def lateral(ref, n):
+        for b in range(depth // zb):
+            lo = reach + b * zb
+            u = ref[n, lo : lo + zb].reshape(zb * X, Y)
+            uh, ul = split(u)
+            acc = jnp.dot(uh, bh_ref[...], preferred_element_type=F32)
+            acc = acc + jnp.dot(kh_ref[...], uh, preferred_element_type=F32)
+            acc = acc + jnp.dot(uh, bl_ref[...], preferred_element_type=F32)
+            acc = acc + jnp.dot(ul, bh_ref[...], preferred_element_type=F32)
+            acc = acc + jnp.dot(kl_ref[...], uh, preferred_element_type=F32)
+            acc = acc + jnp.dot(kh_ref[...], ul, preferred_element_type=F32)
+            ACC[b * zb : (b + 1) * zb] = acc.reshape(zb, X, Y)
 
     barrier = pltpu.get_barrier_semaphore()
     for axis, count in counts.items():
@@ -183,18 +198,20 @@
         return lax.dot_general(lhs, y_hot, (((1,), (1,)), ((), ())), preferred_element_type=F32)
 
     CNT[...] = spread(x_hot.astype(BF16))
+    slab_relay(in_slab(V), vel_state, "dom", "shots")
     for n in range(NF):
         vals = x_hot * obs_ref[0, n : n + 1, :]
-        a, rest = split(vals)
-        b, rest2 = split(vals - a.astype(F32))
-        del rest
-        OB[n] = spread(a) + spread(b) + spread(rest2)
+        a = vals.astype(BF16)
+        b, rest = split(vals - a.astype(F32))
+        OB[n] = spread(a) + spread(b) + spread(rest)
     flat = lax.broadcasted_iota(jnp.int32, (X, Y), 0) * Y + lax.broadcasted_iota(jnp.int32, (X, Y), 1)
     src_hot = (flat == src_ref[0]).astype(F32)
 
-    slab_relay(in_slab(V), vel_state, "dom", "shots")
     field_relay(in_field(U, 1), now_state)
     field_relay(in_whole(SP), sp_state)
+    field_done(in_field(U, 1), now_state)
+    lateral(U, 1)
+    slab_relay_two(in_slab(V), vel_state, "dom", "shots")
     field_relay(in_field(U, 0), prev_state)
     slab_done(in_slab(V), vel_state, "dom", "shots")
     field_done(in_whole(SP), sp_state)
@@ -205,21 +222,7 @@
         QV[z] = (1.0 - damp) * inv
         vel = V[z]
         KP[z] = vel * vel * inv
-    field_done(in_field(U, 1), now_state)
     field_done(in_field(U, 0), prev_state)
-
-    def lateral(ref, n):
-        for b in range(depth // zb):
-            lo = reach + b * zb
-            u = ref[n, lo : lo + zb].reshape(zb * X, Y)
-            uh, ul = split(u)
-            acc = jnp.dot(uh, bh_ref[...], preferred_element_type=F32)
-            acc = acc + jnp.dot(kh_ref[...], uh, preferred_element_type=F32)
-            acc = acc + jnp.dot(uh, bl_ref[...], preferred_element_type=F32)
-            acc = acc + jnp.dot(ul, bh_ref[...], preferred_element_type=F32)
-            acc = acc + jnp.dot(kl_ref[...], uh, preferred_element_type=F32)
-            acc = acc + jnp.dot(kh_ref[...], ul, preferred_element_type=F32)
-            ACC[b * zb : (b + 1) * zb] = acc.reshape(zb, X, Y)
 
     def level(ref, n, z, xr, yr, plane):
         mid = ref[n, reach + z, xr, yr]
@@ -232,57 +235,73 @@
 
     whole_x, whole_y = slice(None), slice(None)
 
-    def advance(ref, n, plane, at):
-        lateral(ref, n)
+    def advance(ref, n, plane, at, ready=False):
+        if not ready:
+            lateral(ref, n)
         for z in range(depth):
             ref[n + 1, reach + z] = level(ref, n, z, whole_x, whole_y, plane if z == at else None)
 
     for n in range(NF):
-        advance(U, n + 1, src_hot * amp_ref[0, n], src_depth)
-        if n == 0:
+        advance(U, n + 1, src_hot * amp_ref[0, n], src_depth, n == 0)
+        if n == max(0, NF - 3):
             field_relay(in_field(L, 1), adj_state)
-        if n == 1:
+        if n == max(0, NF - 2):
             field_relay(in_field(L, 0), adjn_state)
+
+    for z in range(depth):
+        illum = None
+        for n in range(NF):
+            value = U[n + 2, reach + z, own_x, own_y]
+            illum = value * value if illum is None else illum + value * value
+        GI[1, z] = illum
     field_done(in_field(L, 1), adj_state)
+    lateral(L, 1)
+    far_first = sorted(range(1, shots), key=lambda j: -min(j, shots - j))
+
+    def to_owners(f):
+        return [
+            (j, send(GI.at[f, pl.ds(peer("shots", j) * owned, owned)], GR.at[j - 1, f], "shots", j))
+            for j in far_first
+        ]
+
+    illum_parts = to_owners(1)
     field_done(in_field(L, 0), adjn_state)
 
     for n in range(NF, 0, -1):
         plane = CNT[...] * U[n + 1, reach + rec_depth] - OB[n - 1]
-        advance(L, NF + 1 - n, plane, rec_depth)
+        advance(L, NF + 1 - n, plane, rec_depth, n == NF)
 
     for z in range(depth):
         at = (reach + z, own_x, own_y)
         u = [U[(n,) + at] for n in range(NF + 2)]
         grad = None
-        illum = None
         for n in range(NF):
             term = L[(NF + 1 - n,) + at] * (u[n + 2] - 2.0 * u[n + 1] + u[n])
             grad = term if grad is None else grad + term
-            square = u[n + 2] * u[n + 2]
-            illum = square if illum is None else illum + square
         GI[0, z] = grad
-        GI[1, z] = illum
-
-    parts = []
-    for j in range(1, shots):
-        to = peer("shots", j)
-        parts.append(send(GI.at[:, pl.ds(to * owned, owned)], GR.at[j - 1], "shots", j))
+
+    grad_parts = to_owners(0)
     lateral(U, NF + 1)
-    total = GI[:, pl.ds(s * owned, owned)]
-    for j in range(1, shots):
-        arrived(parts[j - 1], GR.at[j - 1], "shots")
-        total = total + GR[j - 1]
-    mine = total[0] / (total[1] + floor_share * shots)
+    below = GI[1, pl.ds(s * owned, owned)] + floor_share * shots
+    for j, idx in illum_parts:
+        arrived(idx, GR.at[j - 1, 1], "shots")
+        below = below + GR[j - 1, 1]
+    above = GI[0, pl.ds(s * owned, owned)]
+    for j, idx in grad_parts:
+        arrived(idx, GR.at[j - 1, 0], "shots")
+        above = above + GR[j - 1, 0]
+    mine = above / below
     PC[pl.ds(s * owned, owned), own_x, own_y] = mine
     pc_state = slab_send(in_slab(PC), "shots", "dom")
     slab_relay(in_slab(PC), pc_state, "shots", "dom")
+    slab_relay_two(in_slab(PC), pc_state, "shots", "dom")
     slab_done(in_slab(PC), pc_state, "shots", "dom")
     top = jnp.abs(PC[0])
     for z in range(1, depth):
         top = jnp.maximum(top, jnp.abs(PC[z]))
     peak = jnp.max(jnp.max(top, axis=0, keepdims=True), axis=1, keepdims=True)
     scale = 1.0 / (peak + 1e-06)
-    dir_ref[...] = mine * scale
+    both_ref[0:owned] = mine * scale
     for z in range(depth):
         updated = V[z] * (1.0 - step_rate * (PC[z] * scale))
         KP[z] = updated * updated * IV[z]
@@ -297,11 +316,17 @@
                 )
         else:
             for z in range(depth):
-                out_ref[0, z] = level(U, NF + 1 + n, z, own_x, own_y, None)
+                both_ref[owned + z] = level(U, NF + 1 + n, z, own_x, own_y, None)
             ACC[0] = plane * IV[src_depth]
-            out_ref[0, src_depth] += ACC[0, own_x, own_y]
+            both_ref[owned + src_depth] += ACC[0, own_x, own_y]
     for copy in sent:
         copy.wait_send()
+
+
+def part(both_ref, dir_ref, out_ref):
+    owned = dir_ref.shape[0]
+    dir_ref[...] = both_ref[0:owned]
+    out_ref[0] = both_ref[owned:]
 
 
 def solution(mesh):
@@ -318,14 +343,11 @@
         sm = pl.BlockSpec(memory_space=pltpu.SMEM)
         whole = pltpu.VMEM((depth, X, Y), F32)
         n_sems = copies_needed(shots, dom, sub)
-        return tuple(pl.pallas_call(
+        both = pl.pallas_call(
             functools.partial(kernel, (shots, dom, sub, depth, rows, cols, owned, zb)),
-            out_shape=(
-                jax.ShapeDtypeStruct((owned, rows, cols), F32),
-                jax.ShapeDtypeStruct((1, depth, rows, cols), F32),
-            ),
+            out_shape=jax.ShapeDtypeStruct((owned + depth, rows, cols), F32),
             in_specs=[vm] * 6 + [sm, sm] + [vm] * 6,
-            out_specs=(vm, vm),
+            out_specs=vm,
             scratch_shapes=[
                 pltpu.VMEM((NF + NFIN + 1, depth + 2 * reach, X, Y), F32),
                 pltpu.VMEM((NF + 2, depth + 2 * reach, X, Y), F32),
@@ -341,7 +363,16 @@
                 collective_id=0, has_side_effects=True, vmem_limit_bytes=56 * 1024 * 1024
             ),
         )(velocity, wave_prev, wave_now, adj_next, adj_now, sponge, wavelet, src_pos, rec_pos, observed,
-          jnp.asarray(bh), jnp.asarray(bl), jnp.asarray(kh), jnp.asarray(kl)))
+          jnp.asarray(bh), jnp.asarray(bl), jnp.asarray(kh), jnp.asarray(kl))
+        return tuple(pl.pallas_call(
+            part,
+            out_shape=(
+                jax.ShapeDtypeStruct((owned, rows, cols), F32),
+                jax.ShapeDtypeStruct((1, depth, rows, cols), F32),
+            ),
+            in_specs=[vm],
+            out_specs=(vm, vm),
+        )(both))
 
     return jax.shard_map(
         shards,

time: 51.6 us -> 46.3 us (0.90)
  local copies, waits for them, and re-layouts: 2.94 us -> 0 us
  Pallas kernels: 47.2 us -> 44.8 us
    pallas_call x1, Pallas kernels: 47.2 us -> 43.2 us  [shards(): pl.pallas_call(functools.partial(kernel, (shots, dom, sub, depth, rows, c...]
    unnamed x2 -> x0, local copies, waits for them, and re-layouts: 2.94 us -> none
    pallas_call x0 -> x1, Pallas kernels: none -> 1.59 us  [shards(): pl.pallas_call(part, out_shape=(jax.ShapeDtypeStruct((owned, rows, cols),...]
where the time goes in v2:
time: 46.3 us; the launch traced here: 46.1 us
  Pallas kernels  44.8 us (97%)
  between operations  1.29 us (3%)
    pallas_call x1, Pallas kernels, shards(): pl.pallas_call(functools.partial(kernel, (shots, dom, sub, depth, rows, c...  43.2 us
    pallas_call x1, Pallas kernels, shards(): pl.pallas_call(part, out_shape=(jax.ShapeDtypeStruct((owned, rows, cols),...  1.59 us

profile of v2, /device:TPU:1, one launch (start us, length us, event | category | flops | bytes accessed | tf_op | source)
XLA Modules:
  0.0 46.1 jit_solution(10034310762399797786)
XLA Ops:
  1.3 43.2 %shard_map.149.both_ref = f32[40,8,128]{2,1,0:T(8,128)} custom-call(f32[8,8,128]{2,1,0:T(8,128)} %vel_ref.1, bf16[1,32,8,128]{3,2,1,0:T(8,128)(2,1)} %prev_ref.1, bf16[1,32,8,128]{3,2,1,0:T(8,128)(2,1)} %now_ref.1, bf16[1,32,8,128]{3,2,1,0:T(8,128)(2,1)} %adjn_ref.1, bf16[1,32,8,128]{3,2,1,0:T(8,128)(2,1)} %adj_ref.1, s32[32,8,128]{2,1,0:T(8,128)} %sponge_ref.1, ...), custom_call_target="tpu_custom_call" | custom-call | tf_op jit(solution)/shard_map/pallas_call | solution.py:346
  44.5 1.6 %shard_map.150 = (f32[8,8,128]{2,1,0:T(8,128)}, f32[1,32,8,128]{3,2,1,0:T(8,128)}) custom-call(f32[40,8,128]{2,1,0:T(8,128)} %shard_map.149.both_ref), custom_call_target="tpu_custom_call" | custom-call | tf_op jit(solution)/shard_map/pallas_call | solution.py:367
